TPU v7x, 512 devices: a whole 4x8x8 slice. The times are simulated.
512 devices in a mesh: leaf: 32 (over z, x), group: 16 (over y, core).
Axes of the slice: x: 4, y: 8, z: 8, core: 2. Of those that a mesh axis runs over, the one named last changes fastest.
Arguments:
- low_solved: float32 [262144, 256], P(('group', 'leaf')), may hold values from -4 to 4, as said below
- low_basis: float32 [262144, 256], P(('group', 'leaf')), may hold values from -0.001933495 to 0.001933495, as said below
- upper_solved: float32 [262144, 512], P(('group', 'leaf')), may hold values from -4 to 4, as said below
- upper_basis: float32 [262144, 256], P(('group', 'leaf')), may hold values from -0.001171875 to 0.001171875, as said below
Outputs:
- pair_solved: float32 [262144, 256], P(('group', 'leaf'))
- next_solved: float32 [262144, 256], P(('group', 'leaf'))
Inputs may be any that keep to these rules, and one draw needn't show every extreme that they name: `low_solved`: independent entries of mean zero. `low_basis`: independent entries of mean zero. `upper_solved`: independent entries of mean zero. `upper_basis`: independent entries of mean zero.
All inputs are finite; a program needn't handle non-finite values.
Results may differ from a plain program's by a relative error of at most 0.0003.
Values sent between devices are 32-bit elements; how exact they have to be, the bound alone decides.
A program may use at most 64 MiB of HBM per device.

v0:
```python
import jax
import jax.numpy as jnp
from jax import lax
from jax.sharding import PartitionSpec as P

ITERS = 4


def partner(x, axis, stride):
    return lax.ppermute(x, axis, [(i, i ^ 1 << stride) for i in range(lax.axis_size(axis))])


def product(left, right):
    return jnp.dot(left, right, precision=lax.Precision.HIGHEST, preferred_element_type=jnp.float32)


def transposed_product(left, right):
    return lax.dot_general(
        left,
        right,
        (((0,), (0,)), ((), ())),
        precision=lax.Precision.HIGHEST,
        preferred_element_type=jnp.float32,
    )


def jacobi(couple_first, rhs_first, couple_second, rhs_second):
    update_first = jnp.zeros(rhs_second.shape, jnp.float32)
    update_second = jnp.zeros(rhs_first.shape, jnp.float32)
    for sweep_index in range(ITERS):
        update_first, update_second = (
            rhs_second - product(couple_second, update_second),
            rhs_first - product(couple_first, update_first),
        )
    return (update_first, update_second)


def body(low_solved, low_basis, upper_solved, upper_basis):
    rank_width = low_solved.shape[1]
    leaves = lax.axis_size("leaf")
    half_index = lax.axis_index("leaf") // (leaves // 2)
    slot_mask = (jnp.arange(2) == half_index).astype(jnp.float32)
    joined = jnp.concatenate([low_solved, upper_solved], axis=1)
    local_terms = transposed_product(low_basis, joined)
    totals = lax.psum(slot_mask[:, None, None] * local_terms[None], "leaf")
    first_half = totals[0]
    second_half = totals[1]
    update_first, update_second = jacobi(
        first_half[:, :rank_width],
        first_half[:, rank_width:],
        second_half[:, :rank_width],
        second_half[:, rank_width:],
    )
    own_update = jnp.where(half_index == 0, update_first, update_second)
    middle = upper_solved - product(low_solved, own_update)
    group_total = lax.psum(transposed_product(upper_basis, middle), "leaf")
    pair_solved = middle[:, :rank_width]
    sibling = partner(group_total, "group", 0)
    parity = lax.axis_index("group") % 2
    first_group = jnp.where(parity == 0, group_total, sibling)
    second_group = jnp.where(parity == 0, sibling, group_total)
    pair_first, pair_second = jacobi(
        first_group[:, :rank_width],
        first_group[:, rank_width:],
        second_group[:, :rank_width],
        second_group[:, rank_width:],
    )
    pair_update = jnp.where(parity == 0, pair_first, pair_second)
    next_solved = middle[:, rank_width:] - product(pair_solved, pair_update)
    return (pair_solved, next_solved)


def solution(mesh):
    return jax.shard_map(
        body,
        mesh=mesh,
        in_specs=(
            P(("group", "leaf"), None),
            P(("group", "leaf"), None),
            P(("group", "leaf"), None),
            P(("group", "leaf"), None),
        ),
        out_specs=(P(("group", "leaf"), None), P(("group", "leaf"), None)),
        check_vma=False,
    )
```

profile of v0, /device:TPU:1, one launch (start us, length us, event | category | flops | bytes accessed | tf_op | source)
XLA Modules:
  0.0 367.2 jit_solution(1575446684602732130)
XLA Ops:
  7.3 1.0 copy-done
  8.2 4.0 %fusion.5 = f32[256,768]{0,1:T(8,128)S(1)} fusion(f32[512,256]{1,0:T(8,128)S(1)} %copy-done, f32[512,512]{1,0:T(8,128)} %param.6, f32[512,256]{1,0:T(8,128)} %param.4), kind=kOutput, calls=%fused_computation.6 | convolution fusion | flops 1208352768 | bytes 2883584 | tf_op jit(solution)/shard_map/dot_general | solution.py:18
  12.5 1.3 broadcast_multiply_fusion
  14.3 164.7 %all-reduce.3.cloned.1.call-done = f32[2,256,768]{2,1,0:T(8,128)} async-done(((f32[2,256,768]{2,1,0:T(8,128)}), f32[2,256,768]{2,1,0:T(8,128)}) %all-reduce.3.cloned.1.call-update) | async-done | bytes 1572880 | tf_op jit(solution)/shard_map/psum | solution.py:45
  179.0 1.5 slice_bitcast_fusion.1
  180.5 0.6 convolution_subtract_fusion.4
  181.0 0.6 convolution_subtract_fusion.8
  181.6 0.6 convolution_subtract_fusion.3
  182.2 0.6 convolution_subtract_fusion.2
  182.9 0.6 convolution_subtract_fusion.7
  183.5 0.6 convolution_subtract_fusion.6
  184.1 0.6 convolution_subtract_fusion.5
  184.8 0.6 fusion.8
  185.4 1.9 fusion.4
  187.3 1.8 convolution_bitcast_fusion.1
  189.1 157.5 %all-reduce.5.cloned.1.call-done = f32[256,512]{0,1:T(8,128)} async-done(((f32[256,512]{0,1:T(8,128)}), f32[256,512]{0,1:T(8,128)}) %all-reduce.5.cloned.1.call-update) | async-done | bytes 524304 | tf_op jit(solution)/shard_map/psum | solution.py:56
  346.6 7.2 %collective-permute-start = (f32[256,512]{0,1:T(8,128)}, f32[256,512]{0,1:T(8,128)S(1)}, u32[]{:S(2)}, u32[]{:S(2)}) collective-permute-start(f32[256,512]{0,1:T(8,128)} %all-reduce.5.cloned.1.call-done), channel_id=1, source_target_pairs={{0,1},{1,0},{2,3},{3,2},{4,5},{5,4},{6,7},{7,6},{8,9},{9,8},{10,11... | collective-permute-start | bytes 1572872 | tf_op jit(solution)/shard_map/ppermute | solution.py:10
  353.9 1.0 copy.9
  354.9 0.5 collective-permute-done
  355.5 0.4 convolution_subtract_fusion.16
  356.3 0.4 convolution_subtract_fusion.15
  358.3 0.4 fusion.9
  358.7 0.6 convolution_subtract_fusion
  359.3 1.0 copy.10
  (23 shorter events, 2.9 us)
Async XLA Ops:
  7.2 1.0 copy-start
  7.2 171.8 %all-reduce.3.cloned.1.call-start = ((), (), s32[]{:S(2)}) async-start(), calls=%async_computation | async-start | bytes 3145728 | tf_op jit(solution)/shard_map/psum | solution.py:45
  12.5 1.5 copy-start.1
  13.8 332.8 %all-reduce.5.cloned.1.call-start = ((), (), s32[]{:S(2)}) async-start(), calls=%async_computation.1 | async-start | bytes 1048576 | tf_op jit(solution)/shard_map/psum | solution.py:56
  184.1 1.3 copy-start.2
  185.4 1.9 copy-start.4
  346.6 8.8 %copy-start.3 = (f32[256,512]{0,1:T(8,128)S(1)}, f32[256,512]{0,1:T(8,128)}, u32[]{:S(2)}) copy-start(f32[256,512]{0,1:T(8,128)} %all-reduce.5.cloned.1.call-done) | copy-start | bytes 1572868
  346.6 8.8 %collective-permute-start = (f32[256,512]{0,1:T(8,128)}, f32[256,512]{0,1:T(8,128)S(1)}, u32[]{:S(2)}, u32[]{:S(2)}) collective-permute-start(f32[256,512]{0,1:T(8,128)} %all-reduce.5.cloned.1.call-done), channel_id=1, source_target_pairs={{0,1},{1,0},{2,3},{3,2},{4,5},{5,4},{6,7},{7,6},{8,9},{9,8},{10,11... | collective-permute-start | bytes 1572872 | tf_op jit(solution)/shard_map/ppermute | solution.py:10
Sparse Core Ops, SparseCore 0:
  13.9 165.0 all-reduce.2
  189.2 157.3 all-reduce.4
where the time goes:
time: 367 us
  waiting for transfers between devices  323 us (88%)
  matrix products  16.3 us (4%)
  between operations  14.3 us (4%)
  starting transfers between devices  7.31 us (2%)
  local copies, waits for them, and re-layouts  5.18 us (1%)
    psum x1, waiting for transfers between devices, body(): totals = lax.psum(slot_mask[:, None, None] * local_terms[None], 'leaf')  165 us
    psum x1, waiting for transfers between devices, body(): group_total = lax.psum(transposed_product(upper_basis, middle), 'leaf')  157 us
    dot_general x18, matrix products, product(): jnp.dot(left, right, precision=lax.Precision.HIGHEST, preferred_element_t...  10.5 us
  transfers between devices with their start and end apart: 3, of which 3 were waited for; matrix products, arithmetic and copies ran while one was open for 0% of the time, Pallas kernels for 0%

commit v1 on v0

--- a/solution.py
+++ b/solution.py
@@ -53,7 +53,7 @@
     )
     own_update = jnp.where(half_index == 0, update_first, update_second)
     middle = upper_solved - product(low_solved, own_update)
-    group_total = lax.psum(transposed_product(upper_basis, middle), "leaf")
+    group_total = jnp.sum(lax.all_gather(transposed_product(upper_basis, middle), "leaf"), axis=0)
     pair_solved = middle[:, :rank_width]
     sibling = partner(group_total, "group", 0)
     parity = lax.axis_index("group") % 2

time: 367 us -> 386 us (1.052)
  local copies, waits for them, and re-layouts: 5.18 us -> 21 us
  other arithmetic: 1.4 us -> 10.1 us
  waiting for transfers between devices: 323 us -> 318 us
    psum x1 -> x0, waiting for transfers between devices: 157 us -> none  [body(): group_total = lax.psum(transposed_product(upper_basis, middle), 'leaf')]
    all_gather x0 -> x1, waiting for transfers between devices: none -> 153 us  [body(): lax.all_gather(transposed_product(upper_basis, middle), 'leaf')]
    unnamed x13 -> x12, local copies, waits for them, and re-layouts: 3.41 us -> 19.2 us
    reduce_sum x0 -> x1, other arithmetic: none -> 8.68 us  [body(): jnp.sum(lax.all_gather(transposed_product(upper_basis, middle), 'leaf'),...]
where the time goes in v1:
time: 386 us
  waiting for transfers between devices  318 us (82%)
  local copies, waits for them, and re-layouts  21 us (5%)
  matrix products  16.3 us (4%)
  between operations  14.3 us (4%)
  other arithmetic  10.1 us (3%)
  starting transfers between devices  5.78 us (1%)
    psum x1, waiting for transfers between devices, body(): totals = lax.psum(slot_mask[:, None, None] * local_terms[None], 'leaf')  165 us
    all_gather x1, waiting for transfers between devices, body(): lax.all_gather(transposed_product(upper_basis, middle), 'leaf')  153 us
    unnamed x12, local copies, waits for them, and re-layouts  19.2 us
    dot_general x18, matrix products, product(): jnp.dot(left, right, precision=lax.Precision.HIGHEST, preferred_element_t...  10.5 us
    reduce_sum x1, other arithmetic, body(): jnp.sum(lax.all_gather(transposed_product(upper_basis, middle), 'leaf'),...  8.68 us
  transfers between devices with their start and end apart: 3, of which 3 were waited for; matrix products, arithmetic and copies ran while one was open for 0% of the time, Pallas kernels for 0%

profile of v1, /device:TPU:1, one launch (start us, length us, event | category | flops | bytes accessed | tf_op | source)
XLA Modules:
  0.0 385.8 jit_solution(11633000419148634014)
XLA Ops:
  7.3 1.0 copy-done
  8.2 4.0 %fusion.5 = f32[256,768]{0,1:T(8,128)S(1)} fusion(f32[512,256]{1,0:T(8,128)S(1)} %copy-done, f32[512,512]{1,0:T(8,128)} %param.6, f32[512,256]{1,0:T(8,128)} %param.4), kind=kOutput, calls=%fused_computation.7 | convolution fusion | flops 1208352768 | bytes 2883584 | tf_op jit(solution)/shard_map/dot_general | solution.py:18
  12.5 1.3 broadcast_multiply_fusion
  14.3 164.7 %all-reduce.2.cloned.1.call-done = f32[2,256,768]{2,1,0:T(8,128)} async-done(((f32[2,256,768]{2,1,0:T(8,128)}), f32[2,256,768]{2,1,0:T(8,128)}) %all-reduce.2.cloned.1.call-update) | async-done | bytes 1572880 | tf_op jit(solution)/shard_map/psum | solution.py:45
  179.0 1.5 slice_bitcast_fusion.1
  180.5 0.6 convolution_subtract_fusion.4
  181.1 0.6 convolution_subtract_fusion.8
  181.6 0.6 convolution_subtract_fusion.3
  182.3 0.6 convolution_subtract_fusion.2
  182.9 0.6 convolution_subtract_fusion.7
  183.5 0.6 convolution_subtract_fusion.6
  184.2 0.6 convolution_subtract_fusion.5
  184.8 0.6 fusion.8
  185.4 1.9 fusion.4
  187.3 1.8 convolution_bitcast_fusion.1
  189.1 153.2 %all-gather.3.cloned.1.call-done = f32[8192,512]{0,1:T(8,128)} async-done(((f32[256,512]{0,1:T(8,128)}), f32[8192,512]{0,1:T(8,128)}) %all-gather.3.cloned.1.call-update) | async-done | bytes 16777232 | tf_op jit(solution)/shard_map/all_gather | solution.py:56
  342.3 15.8 %copy.17 = f32[64,8,32,256]{3,2,1,0:T(8,128)} copy(f32[64,8,32,256]{3,1,2,0:T(8,128)} %bitcast.35) | data formatting | bytes 33554432
  358.1 8.7 %bitcast_reduce_fusion = f32[256,512]{0,1:T(8,128)S(1)} fusion(f32[64,8,32,256]{3,2,1,0:T(8,128)} %copy.17), kind=kLoop, calls=%fused_computation | loop fusion | flops 4063232 | bytes 17301504 | tf_op jit(solution)/shard_map/reduce_sum | solution.py:56
  366.8 5.7 %collective-permute-start = (f32[256,512]{0,1:T(8,128)S(1)}, f32[256,512]{0,1:T(8,128)S(1)}, u32[]{:S(2)}, u32[]{:S(2)}) collective-permute-start(f32[256,512]{0,1:T(8,128)S(1)} %bitcast_reduce_fusion), channel_id=1, source_target_pairs={{0,1},{1,0},{2,3},{3,2},{4,5},{5,4},{6,7},{7,6},{8,9},{9,8},{10,11... | collective-permute-start | bytes 1572872 | tf_op jit(solution)/shard_map/ppermute | solution.py:10
  372.6 1.0 copy.14
  373.6 0.5 collective-permute-done
  376.9 0.4 fusion.9
  377.3 0.6 convolution_subtract_fusion
  378.0 1.0 copy.15
  (23 shorter events, 3.7 us)
Async XLA Ops:
  7.2 1.0 copy-start
  7.2 171.8 %all-reduce.2.cloned.1.call-start = ((), (), s32[]{:S(2)}) async-start(), calls=%async_computation | async-start | bytes 3145728 | tf_op jit(solution)/shard_map/psum | solution.py:45
  12.5 1.5 copy-start.1
  13.8 328.5 %all-gather.3.cloned.1.call-start = ((), (), s32[]{:S(2)}) async-start(), calls=%async_computation.1 | async-start | bytes 17301504 | tf_op jit(solution)/shard_map/all_gather | solution.py:56
  184.1 1.3 copy-start.2
  185.4 1.9 copy-start.3
  366.8 7.2 %collective-permute-start = (f32[256,512]{0,1:T(8,128)S(1)}, f32[256,512]{0,1:T(8,128)S(1)}, u32[]{:S(2)}, u32[]{:S(2)}) collective-permute-start(f32[256,512]{0,1:T(8,128)S(1)} %bitcast_reduce_fusion), channel_id=1, source_target_pairs={{0,1},{1,0},{2,3},{3,2},{4,5},{5,4},{6,7},{7,6},{8,9},{9,8},{10,11... | collective-permute-start | bytes 1572872 | tf_op jit(solution)/shard_map/ppermute | solution.py:10
Sparse Core Ops, SparseCore 0:
  13.9 165.0 all-reduce.1
  189.2 153.0 all-gather.2
